TPU v7x, 32 devices: a whole 2x2x4 slice. The times are simulated.
32 devices in a mesh: ctx: 16 (over z, x, core), vocab: 2 (over y).
Axes of the slice: x: 2, y: 2, z: 4, core: 2. Of those that a mesh axis runs over, the one named last changes fastest.
Arguments:
- hidden: bfloat16 [4096, 8192], P('ctx', 'vocab'), may hold values from -540 to 540
- norm_gain: float32 [8192], P('vocab'), may hold values from 0.5 to 1.5
- head: bfloat16 [15808, 8192], P('ctx', 'vocab'), may hold values from -0.53033009 to 0.53033009
- masked_pos: int32 [2, 16], replicated, may hold values from 0 to 2047, as said below
- masked_targets: int32 [2, 16], replicated, may hold values from 0 to 15807
- t_num: int32 [2], replicated, may hold values from 1 to 3, as said below
- t_den: int32 [2], replicated, may hold values from 192 to 319
Outputs:
- loss_value: float32 [], replicated
- grad_hidden: bfloat16 [4096, 8192], P('ctx', 'vocab')
- grad_head: bfloat16 [15808, 8192], P('ctx', 'vocab')
- grad_gain: float32 [8192], P('vocab')
Inputs may be any that keep to these rules, and one draw needn't show every extreme that they name: `masked_pos`: each row lists 16 distinct positions of one sequence in increasing order; at most 8 of them fall in one aligned block of 256 positions, and exactly 8 in some blocks of every sequence. `t_num`: the two numerators differ.
All inputs are finite; a program needn't handle non-finite values.
Results may differ from a plain program's by a relative error of at most 0.0081.
Values may be sent and summed in bfloat16 or wider, within the bound.
No kernel may reach another device: no remote copies, remote signals or barrier semaphores. Data moves between devices by JAX's collectives and lax.ppermute only.
A program may use at most 64 MiB of HBM per device.

v0:
```python
import jax
import jax.numpy as jnp
from jax import lax
from jax.sharding import PartitionSpec as P

CAP = 8
EPSILON = 1e-05
LOSS_SCALE = 1024.0


def joined(part, axis, combine):
    gathered = jax.tree.map(lambda a: lax.all_gather(a, axis), part)

    def take(source):
        return jax.tree.map(lambda a: lax.dynamic_index_in_dim(a, source, 0, False), gathered)

    return lax.fori_loop(
        1, lax.axis_size(axis), lambda source, state: combine(state, take(source)), take(0)
    )


def contract_last(left, right):
    return lax.dot_general(
        left, right, (((1,), (1,)), ((), ())), preferred_element_type=jnp.float32
    )


def combine_stats(first, second):
    row_top = jnp.maximum(first[0], second[0])
    exp_total = first[1] * jnp.exp(first[0] - row_top) + second[1] * jnp.exp(second[0] - row_top)
    return (row_top, exp_total, first[2] + second[2])


def on_device(hidden, norm_gain, head, masked_pos, masked_targets, t_num, t_den):
    tok_here, width_here = hidden.shape
    voc_here = head.shape[0]
    ctx_count = lax.axis_size("ctx")
    vocab_count = lax.axis_size("vocab")
    ctx_index = lax.axis_index("ctx")
    vocab_index = lax.axis_index("vocab")
    blocks = ctx_count // 2
    slot_count = masked_pos.shape[1]
    model_width = width_here * vocab_count
    seq_here = ctx_index // blocks
    block_here = ctx_index % blocks
    block_of = masked_pos // tok_here
    block_ids = jnp.arange(blocks, dtype=jnp.int32)
    counts = jnp.sum((block_of[:, :, None] == block_ids[None, None, :]).astype(jnp.int32), axis=1)
    offsets = jnp.cumsum(counts, axis=1) - counts
    weight = t_den.astype(jnp.float32) / (t_num.astype(jnp.float32) * (2.0 * tok_here * blocks))
    lane_ids = jnp.arange(CAP, dtype=jnp.int32)
    own_count = counts[seq_here, block_here]
    own_start = offsets[seq_here, block_here]
    own_valid = lane_ids < own_count
    seq_list = jnp.concatenate([masked_pos[seq_here], jnp.zeros((CAP,), jnp.int32)])
    own_pos = lax.dynamic_slice_in_dim(seq_list, own_start, CAP) - block_here * tok_here
    own_pos = jnp.where(own_valid, own_pos, 0)
    own_rows = jnp.where(own_valid[:, None], hidden[own_pos].astype(jnp.float32), 0.0)
    squares = lax.psum(jnp.sum(own_rows * own_rows, axis=1), "vocab")
    inverse = lax.rsqrt(squares / model_width + EPSILON)
    normed_own = (own_rows * inverse[:, None] * norm_gain[None, :]).astype(jnp.bfloat16)
    normed_all = lax.all_gather(normed_own, "ctx", axis=0, tiled=True)
    row_ids = jnp.arange(ctx_count * CAP, dtype=jnp.int32)
    owner_ctx = row_ids // CAP
    lane_of = row_ids % CAP
    owner_seq = owner_ctx // blocks
    owner_block = owner_ctx % blocks
    row_valid = lane_of < counts[owner_seq, owner_block]
    list_slot = jnp.minimum(offsets[owner_seq, owner_block] + lane_of, slot_count - 1)
    row_targets = masked_targets[owner_seq, list_slot]
    row_factor = jnp.where(row_valid, weight[owner_seq], 0.0)
    row_total = normed_all.shape[0]
    rows_block = row_total // vocab_count
    logits = lax.psum_scatter(
        contract_last(normed_all, head), "vocab", scatter_dimension=0, tiled=True
    )
    block_start = vocab_index * rows_block
    target_cols = (
        lax.dynamic_slice_in_dim(row_targets, block_start, rows_block) - ctx_index * voc_here
    )
    factor = lax.dynamic_slice_in_dim(row_factor, block_start, rows_block)
    columns = jnp.arange(voc_here, dtype=jnp.int32)
    is_target = columns[None, :] == target_cols[:, None]
    picked = jnp.sum(jnp.where(is_target, logits, 0.0), axis=1)
    local_top = jnp.max(logits, axis=1)
    local_total = jnp.sum(jnp.exp(logits - local_top[:, None]), axis=1)
    row_top, exp_total, picked = joined((local_top, local_total, picked), "ctx", combine_stats)
    log_total = row_top + jnp.log(exp_total)
    loss_value = lax.psum(jnp.sum(factor * (log_total - picked)), "vocab")
    softmax_out = jnp.exp(logits - log_total[:, None])
    dlogits = (
        (LOSS_SCALE * factor)[:, None] * (softmax_out - is_target.astype(jnp.float32))
    ).astype(jnp.bfloat16)
    all_grads = lax.all_gather(dlogits, "vocab", axis=0, tiled=True)
    grad_head = lax.dot_general(
        all_grads, normed_all, (((0,), (0,)), ((), ())), preferred_element_type=jnp.float32
    ).astype(jnp.bfloat16)
    own_grad = lax.psum_scatter(
        jnp.dot(all_grads, head, preferred_element_type=jnp.float32),
        "ctx",
        scatter_dimension=0,
        tiled=True,
    )
    own_grad = jnp.where(own_valid[:, None], own_grad, 0.0)
    grad_gain = lax.psum(jnp.sum(own_grad * own_rows * inverse[:, None], axis=0), "ctx")
    inner_mean = (
        lax.psum(jnp.sum(norm_gain[None, :] * own_grad * own_rows, axis=1), "vocab") / model_width
    )
    row_grads = (
        inverse[:, None] * norm_gain[None, :] * own_grad
        - own_rows * (inverse * inverse * inverse * inner_mean)[:, None]
    )
    write_rows = jnp.where(own_valid, own_pos, tok_here)
    grad_hidden = (
        jnp.zeros((tok_here, width_here), jnp.bfloat16)
        .at[write_rows]
        .set(row_grads.astype(jnp.bfloat16), mode="drop")
    )
    return (loss_value, grad_hidden, grad_head, grad_gain)


def solution(mesh):
    placed = (P("ctx", "vocab"), P("vocab"), P("ctx", "vocab"), P(), P(), P(), P())
    return jax.shard_map(
        on_device,
        mesh=mesh,
        in_specs=placed,
        out_specs=(P(), P("ctx", "vocab"), P("ctx", "vocab"), P("vocab")),
        check_vma=False,
    )
```

profile of v0, /device:TPU:0, one launch (start us, length us, event | category | flops | bytes accessed | tf_op | source)
XLA Modules:
  0.0 292.8 jit_solution(3344552635716309176)
XLA Ops:
  7.2 0.0 all-gather.5.cloned.1.call-start
  7.3 0.8 and_select_fusion.4
  8.1 0.1 convert_reduce_fusion
  8.3 0.2 reduce_window_sum.11
  8.4 0.7 dynamic-slice_bitcast_fusion
  9.1 0.6 dynamic_slice.59
  9.7 0.6 dynamic_slice.61
  11.6 0.7 iota_compare_fusion.2
  12.9 0.7 compare_select_fusion
  13.7 0.6 gather_fusion.1
  14.3 0.2 multiply_reduce_fusion.2
  14.5 5.9 %psum.28 = f32[8]{0:T(128)S(1)} all-reduce(f32[8]{0:T(128)S(1)} %multiply_reduce_fusion.2), channel_id=1, replica_groups=mesh['ctx'=16,'vocab'=2] {'vocab'}, use_global_device_ids=true, to_apply=%region_3.4 | all-reduce | flops 8 | bytes 64 | tf_op jit(solution)/shard_map/psum | solution.py:59
  20.4 1.4 multiply_convert_fusion.1
  21.8 0.0 all-gather.5.cloned.1.call-update
  21.8 0.0 reduce-scatter.3.cloned.1.call-start
  21.9 39.7 %all-gather.5.cloned.1.call-done = bf16[128,4096]{1,0:T(8,128)(2,1)} async-done(((bf16[8,4096]{1,0:T(8,128)(2,1)}), bf16[128,4096]{1,0:T(8,128)(2,1)}) %all-gather.5.cloned.1.call-update) | async-done | bytes 1048592 | tf_op jit(solution)/shard_map/all_gather | solution.py:62
  61.6 7.1 %fusion.28 = f32[128,988]{1,0:T(8,128)} fusion(bf16[128,4096]{1,0:T(8,128)(2,1)} %all-gather.5.cloned.1.call-done, bf16[988,4096]{1,0:T(8,128)(2,1)} %param.11), kind=kOutput, calls=%fused_computation.82 | convolution fusion | flops 1035993088 | bytes 9648128 | tf_op jit(solution)/shard_map/dot_general | solution.py:23
  68.7 0.0 reduce-scatter.3.cloned.1.call-update
  68.7 0.0 reduce-scatter.5.cloned.1.call-start
  68.8 1.5 gather_fusion.2
  70.3 1.5 gather_fusion
  71.9 1.5 gather_fusion.3
  73.4 0.6 dynamic-slice
  74.6 0.1 dynamic-slice_subtract_fusion
  74.7 0.6 fusion.27
  75.3 1.3 compare_select_fusion.6
  76.6 5.8 %reduce-scatter.3.cloned.1.call-done = f32[64,988]{1,0:T(8,128)} async-done(((f32[128,988]{1,0:T(8,128)}), f32[64,988]{1,0:T(8,128)}) %reduce-scatter.3.cloned.1.call-update) | async-done | bytes 252944 | tf_op jit(solution)/shard_map/reduce_scatter | solution.py:74
  82.4 1.1 reduce_max.9
  83.5 0.2 dynamic-update-slice
  83.8 1.2 select_reduce_fusion
  85.0 0.2 dynamic-update-slice.2
  85.2 0.2 dynamic-update-slice.1
  85.4 61.0 %all-reduce.4 = (f32[1024]{0:T(1024)S(1)}, f32[1024]{0:T(1024)S(1)}, f32[1024]{0:T(1024)S(1)}) all-reduce(f32[1024]{0:T(1024)S(1)} %dynamic-update-slice, f32[1024]{0:T(1024)S(1)} %dynamic-update-slice.1, f32[1024]{0:T(1024)S(1)} %dynamic-update-slice.2), channel_id=2, replica_groups=mesh['ctx'=16,'vocab'=2] {'ctx'}, use_global_device_ids=true, to_apply=%add.1 | all-reduce | flops 3072 | bytes 24576
  146.4 0.1 reshape.215
  146.5 0.1 reshape.216
  146.6 0.1 reshape.217
  146.6 0.7 while.19
  147.3 0.7 multiply_reduce_fusion.3
  148.0 1.1 multiply_convert_fusion
  149.1 5.6 %all_gather.31 = bf16[128,988]{1,0:T(8,128)(2,1)S(1)} all-gather(bf16[64,988]{1,0:T(8,128)(2,1)S(1)} %multiply_convert_fusion), channel_id=1, replica_groups=mesh['ctx'=16,'vocab'=2] {'vocab'}, dimensions={0}, use_global_device_ids=true | all-gather | bytes 379392 | tf_op jit(solution)/shard_map/all_gather | solution.py:94
  154.8 6.0 %fusion.29 = f32[128,4096]{1,0:T(8,128)} fusion(bf16[128,988]{1,0:T(8,128)(2,1)S(1)} %all_gather.31, bf16[988,4096]{1,0:T(8,128)(2,1)} %param.11), kind=kOutput, calls=%fused_computation.83 | convolution fusion | flops 1035993088 | bytes 10443776 | tf_op jit(solution)/shard_map/dot_general | solution.py:99
  160.8 0.0 reduce-scatter.5.cloned.1.call-update
  160.8 5.6 %convolution_convert_fusion = bf16[988,4096]{1,0:T(8,128)(2,1)} fusion(bf16[128,988]{1,0:T(8,128)(2,1)S(1)} %all_gather.31, bf16[128,4096]{1,0:T(8,128)(2,1)S(1)} %copy-done.2), kind=kOutput, calls=%fused_computation.15 | convolution fusion | flops 1040039936 | bytes 9395200 | tf_op jit(solution)/shard_map/dot_general | solution.py:95
  166.4 52.7 %reduce-scatter.5.cloned.1.call-done = f32[8,4096]{1,0:T(8,128)} async-done(((f32[128,4096]{1,0:T(8,128)}), f32[8,4096]{1,0:T(8,128)}) %reduce-scatter.5.cloned.1.call-update) | async-done | bytes 131088 | tf_op jit(solution)/shard_map/reduce_scatter | solution.py:98
  219.1 1.2 multiply_reduce_fusion
  220.2 5.6 %all-reduce.5 = (f32[]{:T(128)}, f32[8]{0:T(128)S(1)}) all-reduce(f32[]{:T(128)} %get-tuple-element.212, f32[8]{0:T(128)S(1)} %get-tuple-element.188), channel_id=1, replica_groups=mesh['ctx'=16,'vocab'=2] {'vocab'}, use_global_device_ids=true, to_apply=%region_11.12 | all-reduce | flops 9 | bytes 72 | tf_op jit(solution)/shard_map/psum | solution.py:89
  225.8 57.6 %psum.31 = f32[4096]{0:T(1024)} all-reduce(f32[4096]{0:T(1024)S(1)} %get-tuple-element.187), channel_id=1, replica_groups=mesh['ctx'=16,'vocab'=2] {'ctx'}, use_global_device_ids=true, to_apply=%region_17.18 | all-reduce | flops 4096 | bytes 32768 | tf_op jit(solution)/shard_map/psum | solution.py:105
  283.4 2.9 scatter_custom_fusion
  (43 shorter events, 0.6 us)
Async XLA Ops:
  7.2 6.5 %copy-start = (bf16[256,4096]{1,0:T(8,128)(2,1)S(1)}, bf16[256,4096]{1,0:T(8,128)(2,1)}, u32[]{:S(2)}) copy-start(bf16[256,4096]{1,0:T(8,128)(2,1)} %param.9) | copy-start | bytes 6291460
  7.2 66.2 %copy-start.6 = (u32[32]{0:T(128)S(1)}, u32[32]{0:T(128)}, u32[]{:S(2)}) copy-start(u32[32]{0:T(128)} %constant.218) | copy-start | bytes 388
  7.2 64.7 %copy-start.1 = (s32[2,16]{1,0:T(2,128)S(1)}, s32[2,16]{1,0:T(2,128)}, u32[]{:S(2)}) copy-start(s32[2,16]{1,0:T(2,128)} %param.13) | copy-start | bytes 388
  7.2 67.5 %copy-start.4 = (s32[2]{0:T(128)S(1)}, s32[2]{0:T(128)}, u32[]{:S(2)}) copy-start(s32[2]{0:T(128)} %param.14) | copy-start | bytes 28
  7.2 67.5 %copy-start.5 = (s32[2]{0:T(128)S(1)}, s32[2]{0:T(128)}, u32[]{:S(2)}) copy-start(s32[2]{0:T(128)} %param.15) | copy-start | bytes 28
  7.2 54.4 %all-gather.5.cloned.1.call-start = ((), (), s32[]{:S(2)}) async-start(), calls=%async_computation.2 | async-start | bytes 1114112 | tf_op jit(solution)/shard_map/all_gather | solution.py:62
  21.8 60.6 %reduce-scatter.3.cloned.1.call-start = ((), (), s32[]{:S(2)}) async-start(), calls=%async_computation.3 | async-start | bytes 786432 | tf_op jit(solution)/shard_map/reduce_scatter | solution.py:74
  68.7 150.4 %reduce-scatter.5.cloned.1.call-start = ((), (), s32[]{:S(2)}) async-start(), calls=%async_computation.4 | async-start | bytes 2228224 | tf_op jit(solution)/shard_map/reduce_scatter | solution.py:98
  154.8 6.0 %copy-start.2 = (bf16[128,4096]{1,0:T(8,128)(2,1)S(1)}, bf16[128,4096]{1,0:T(8,128)(2,1)}, u32[]{:S(2)}) copy-start(bf16[128,4096]{1,0:T(8,128)(2,1)} %all-gather.5.cloned.1.call-done) | copy-start | bytes 3145732
  160.8 58.3 %copy-start.3 = (f32[4096]{0:T(1024)S(1)}, f32[4096]{0:T(1024)}, u32[]{:S(2)}) copy-start(f32[4096]{0:T(1024)} %param.10) | copy-start | bytes 49156
Sparse Core Ops, SparseCore 0:
  22.0 39.5 all-gather.4
  68.8 13.5 reduce-scatter.2
  160.9 58.1 reduce-scatter.4
where the time goes:
time: 293 us
  blocking collectives  136 us (46%)
  waiting for transfers between devices  98.2 us (34%)
  matrix products  18.7 us (6%)
  between operations  16.6 us (6%)
  other arithmetic  14.1 us (5%)
  local copies, waits for them, and re-layouts  9.14 us (3%)
    unnamed x1, blocking collectives  61 us
    psum x1, blocking collectives, on_device(): lax.psum(jnp.sum(own_grad * own_rows * inverse[:, None], axis=0), 'ctx')  57.6 us
    reduce_scatter x1, waiting for transfers between devices, on_device(): lax.psum_scatter(jnp.dot(all_grads, head, preferred_element_type=jnp.floa...  52.7 us
    all_gather x1, waiting for transfers between devices, on_device(): normed_all = lax.all_gather(normed_own, 'ctx', axis=0, tiled=True)  39.7 us
    dot_general x1, matrix products, contract_last(): lax.dot_general(left, right, (((1,), (1,)), ((), ())), preferred_element_...  7.06 us
    dot_general x1, matrix products, on_device(): jnp.dot(all_grads, head, preferred_element_type=jnp.float32)  5.98 us
    psum x1, blocking collectives, on_device(): squares = lax.psum(jnp.sum(own_rows * own_rows, axis=1), 'vocab')  5.89 us
  transfers between devices with their start and end apart: 3, of which 3 were waited for; matrix products, arithmetic and copies ran while one was open for 4% of the time, Pallas kernels for 0%

commit v1 on v0

--- a/solution.py
+++ b/solution.py
@@ -59,7 +59,14 @@
     squares = lax.psum(jnp.sum(own_rows * own_rows, axis=1), "vocab")
     inverse = lax.rsqrt(squares / model_width + EPSILON)
     normed_own = (own_rows * inverse[:, None] * norm_gain[None, :]).astype(jnp.bfloat16)
-    normed_all = lax.all_gather(normed_own, "ctx", axis=0, tiled=True)
+    size = lax.axis_size("ctx")
+    forward = [(i, (i + 1) % size) for i in range(size)]
+    pieces = [normed_own]
+    for far in range(1, size):
+        pieces = [lax.ppermute(pieces[0], "ctx", forward), *pieces]
+    result = jnp.concatenate(pieces, axis=0)
+    shift = (lax.axis_index("ctx") + 1) * pieces[-1].shape[0]
+    normed_all = jnp.roll(result, shift, axis=0)
     row_ids = jnp.arange(ctx_count * CAP, dtype=jnp.int32)
     owner_ctx = row_ids // CAP
     lane_of = row_ids % CAP

time: 293 us -> 350 us (1.19)
  waiting for transfers between devices: 98.2 us -> 152 us
    ppermute x0 -> x15, waiting for transfers between devices: none -> 95.8 us  [on_device(): pieces = [lax.ppermute(pieces[0], 'ctx', forward), *pieces]]
    all_gather x1 -> x0, waiting for transfers between devices: 39.7 us -> none  [on_device(): normed_all = lax.all_gather(normed_own, 'ctx', axis=0, tiled=True)]
  transfers between devices with their start and end apart: 3 -> 17, of which waited for: 3 -> 17; matrix products, arithmetic and copies ran while one was open for 4% -> 4% of each run, Pallas kernels for 0% -> 0%
where the time goes in v1:
time: 350 us; the launch traced here: 349 us
  waiting for transfers between devices  152 us (43%)
  blocking collectives  136 us (39%)
  matrix products  19.5 us (6%)
  between operations  17.1 us (5%)
  other arithmetic  13.6 us (4%)
  local copies, waits for them, and re-layouts  10.7 us (3%)
    ppermute x15, waiting for transfers between devices, on_device(): pieces = [lax.ppermute(pieces[0], 'ctx', forward), *pieces]  95.8 us
    unnamed x1, blocking collectives  61.1 us
    psum x1, blocking collectives, on_device(): lax.psum(jnp.sum(own_grad * own_rows * inverse[:, None], axis=0), 'ctx')  57.6 us
    reduce_scatter x1, waiting for transfers between devices, on_device(): lax.psum_scatter(jnp.dot(all_grads, head, preferred_element_type=jnp.floa...  51.3 us
  transfers between devices with their start and end apart: 17, of which 17 were waited for; matrix products, arithmetic and copies ran while one was open for 4% of the time, Pallas kernels for 0%

profile of v1, /device:TPU:0, one launch (start us, length us, event | category | flops | bytes accessed | tf_op | source)
XLA Modules:
  0.0 349.0 jit_solution(2692927793039947385)
XLA Ops:
  7.3 0.8 and_select_fusion.4
  8.4 0.7 dynamic-slice_bitcast_fusion
  9.1 0.6 dynamic_slice.63
  9.7 0.6 dynamic_slice.65
  11.6 0.7 iota_compare_fusion.2
  12.9 0.7 compare_select_fusion
  13.6 0.6 gather_fusion.1
  14.4 5.9 %psum.28 = f32[8]{0:T(128)S(1)} all-reduce(f32[8]{0:T(128)S(1)} %multiply_reduce_fusion.2), channel_id=1, replica_groups=mesh['ctx'=16,'vocab'=2] {'vocab'}, use_global_device_ids=true, to_apply=%region_3.4 | all-reduce | flops 8 | bytes 64 | tf_op jit(solution)/shard_map/psum | solution.py:59
  20.3 0.8 multiply_convert_fusion.1
  21.2 6.4 %collective-permute-done = bf16[8,4096]{1,0:T(8,128)(2,1)S(1)} collective-permute-done((bf16[8,4096]{1,0:T(8,128)(2,1)S(1)}, bf16[8,4096]{1,0:T(8,128)(2,1)S(1)}, u32[]{:S(2)}, u32[]{:S(2)}) %collective-permute-start) | collective-permute-done | bytes 65568 | tf_op jit(solution)/shard_map/ppermute | solution.py:66
  27.6 6.4 %collective-permute-done.1 = bf16[8,4096]{1,0:T(8,128)(2,1)S(1)} collective-permute-done((bf16[8,4096]{1,0:T(8,128)(2,1)S(1)}, bf16[8,4096]{1,0:T(8,128)(2,1)S(1)}, u32[]{:S(2)}, u32[]{:S(2)}) %collective-permute-start.1) | collective-permute-done | bytes 65568 | tf_op jit(solution)/shard_map/ppermute | solution.py:66
  34.0 6.4 %collective-permute-done.2 = bf16[8,4096]{1,0:T(8,128)(2,1)S(1)} collective-permute-done((bf16[8,4096]{1,0:T(8,128)(2,1)S(1)}, bf16[8,4096]{1,0:T(8,128)(2,1)S(1)}, u32[]{:S(2)}, u32[]{:S(2)}) %collective-permute-start.2) | collective-permute-done | bytes 65568 | tf_op jit(solution)/shard_map/ppermute | solution.py:66
  40.4 6.4 %collective-permute-done.3 = bf16[8,4096]{1,0:T(8,128)(2,1)S(1)} collective-permute-done((bf16[8,4096]{1,0:T(8,128)(2,1)S(1)}, bf16[8,4096]{1,0:T(8,128)(2,1)S(1)}, u32[]{:S(2)}, u32[]{:S(2)}) %collective-permute-start.3) | collective-permute-done | bytes 65568 | tf_op jit(solution)/shard_map/ppermute | solution.py:66
  46.8 6.4 %collective-permute-done.4 = bf16[8,4096]{1,0:T(8,128)(2,1)S(1)} collective-permute-done((bf16[8,4096]{1,0:T(8,128)(2,1)S(1)}, bf16[8,4096]{1,0:T(8,128)(2,1)S(1)}, u32[]{:S(2)}, u32[]{:S(2)}) %collective-permute-start.4) | collective-permute-done | bytes 65568 | tf_op jit(solution)/shard_map/ppermute | solution.py:66
  53.2 6.4 %collective-permute-done.5 = bf16[8,4096]{1,0:T(8,128)(2,1)S(1)} collective-permute-done((bf16[8,4096]{1,0:T(8,128)(2,1)S(1)}, bf16[8,4096]{1,0:T(8,128)(2,1)S(1)}, u32[]{:S(2)}, u32[]{:S(2)}) %collective-permute-start.5) | collective-permute-done | bytes 65568 | tf_op jit(solution)/shard_map/ppermute | solution.py:66
  59.5 6.4 %collective-permute-done.6 = bf16[8,4096]{1,0:T(8,128)(2,1)S(1)} collective-permute-done((bf16[8,4096]{1,0:T(8,128)(2,1)S(1)}, bf16[8,4096]{1,0:T(8,128)(2,1)S(1)}, u32[]{:S(2)}, u32[]{:S(2)}) %collective-permute-start.6) | collective-permute-done | bytes 65568 | tf_op jit(solution)/shard_map/ppermute | solution.py:66
  65.9 6.4 %collective-permute-done.7 = bf16[8,4096]{1,0:T(8,128)(2,1)S(1)} collective-permute-done((bf16[8,4096]{1,0:T(8,128)(2,1)S(1)}, bf16[8,4096]{1,0:T(8,128)(2,1)S(1)}, u32[]{:S(2)}, u32[]{:S(2)}) %collective-permute-start.7) | collective-permute-done | bytes 65568 | tf_op jit(solution)/shard_map/ppermute | solution.py:66
  72.3 6.4 %collective-permute-done.8 = bf16[8,4096]{1,0:T(8,128)(2,1)S(1)} collective-permute-done((bf16[8,4096]{1,0:T(8,128)(2,1)S(1)}, bf16[8,4096]{1,0:T(8,128)(2,1)S(1)}, u32[]{:S(2)}, u32[]{:S(2)}) %collective-permute-start.8) | collective-permute-done | bytes 65568 | tf_op jit(solution)/shard_map/ppermute | solution.py:66
  78.7 6.4 %collective-permute-done.9 = bf16[8,4096]{1,0:T(8,128)(2,1)S(1)} collective-permute-done((bf16[8,4096]{1,0:T(8,128)(2,1)S(1)}, bf16[8,4096]{1,0:T(8,128)(2,1)S(1)}, u32[]{:S(2)}, u32[]{:S(2)}) %collective-permute-start.9) | collective-permute-done | bytes 65568 | tf_op jit(solution)/shard_map/ppermute | solution.py:66
  85.1 6.4 %collective-permute-done.10 = bf16[8,4096]{1,0:T(8,128)(2,1)S(1)} collective-permute-done((bf16[8,4096]{1,0:T(8,128)(2,1)S(1)}, bf16[8,4096]{1,0:T(8,128)(2,1)S(1)}, u32[]{:S(2)}, u32[]{:S(2)}) %collective-permute-start.10) | collective-permute-done | bytes 65568 | tf_op jit(solution)/shard_map/ppermute | solution.py:66
  91.5 6.4 %collective-permute-done.11 = bf16[8,4096]{1,0:T(8,128)(2,1)S(1)} collective-permute-done((bf16[8,4096]{1,0:T(8,128)(2,1)S(1)}, bf16[8,4096]{1,0:T(8,128)(2,1)S(1)}, u32[]{:S(2)}, u32[]{:S(2)}) %collective-permute-start.11) | collective-permute-done | bytes 65568 | tf_op jit(solution)/shard_map/ppermute | solution.py:66
  97.9 6.4 %collective-permute-done.12 = bf16[8,4096]{1,0:T(8,128)(2,1)S(1)} collective-permute-done((bf16[8,4096]{1,0:T(8,128)(2,1)S(1)}, bf16[8,4096]{1,0:T(8,128)(2,1)S(1)}, u32[]{:S(2)}, u32[]{:S(2)}) %collective-permute-start.12) | collective-permute-done | bytes 65568 | tf_op jit(solution)/shard_map/ppermute | solution.py:66
  104.3 6.4 %collective-permute-done.13 = bf16[8,4096]{1,0:T(8,128)(2,1)S(1)} collective-permute-done((bf16[8,4096]{1,0:T(8,128)(2,1)S(1)}, bf16[8,4096]{1,0:T(8,128)(2,1)S(1)}, u32[]{:S(2)}, u32[]{:S(2)}) %collective-permute-start.13) | collective-permute-done | bytes 65568 | tf_op jit(solution)/shard_map/ppermute | solution.py:66
  110.7 6.4 %collective-permute-done.14 = bf16[8,4096]{1,0:T(8,128)(2,1)S(1)} collective-permute-done((bf16[8,4096]{1,0:T(8,128)(2,1)S(1)}, bf16[8,4096]{1,0:T(8,128)(2,1)S(1)}, u32[]{:S(2)}, u32[]{:S(2)}) %collective-permute-start.14) | collective-permute-done | bytes 65568 | tf_op jit(solution)/shard_map/ppermute | solution.py:66
  117.7 1.3 copy-done.2
  119.0 6.7 %fusion.10 = f32[128,988]{1,0:T(8,128)} fusion(bf16[988,4096]{1,0:T(8,128)(2,1)} %param.11, bf16[256,4096]{1,0:T(8,128)(2,1)S(1)} %constant_dynamic-update-slice_fusion, s32[]{:T(128)S(6)} %select_n.206), kind=kOutput, calls=%fused_computation.19 | convolution fusion | flops 1035993088 | bytes 9648132 | tf_op jit(solution)/shard_map/dot_general | solution.py:23
  125.9 1.5 gather_fusion.2
  127.4 1.5 gather_fusion
  129.0 1.5 gather_fusion.3
  130.5 0.6 dynamic-slice
  131.8 0.6 fusion.32
  132.4 1.2 compare_select_fusion.6
  133.7 4.7 %reduce-scatter.3.cloned.1.call-done = f32[64,988]{1,0:T(8,128)} async-done(((f32[128,988]{1,0:T(8,128)}), f32[64,988]{1,0:T(8,128)}) %reduce-scatter.3.cloned.1.call-update) | async-done | bytes 252944 | tf_op jit(solution)/shard_map/reduce_scatter | solution.py:81
  138.4 1.1 reduce_max.9
  139.7 1.2 select_reduce_fusion
  140.9 0.2 dynamic-update-slice.2
  141.4 61.1 %all-reduce.4 = (f32[1024]{0:T(1024)S(1)}, f32[1024]{0:T(1024)S(1)}, f32[1024]{0:T(1024)S(1)}) all-reduce(f32[1024]{0:T(1024)S(1)} %dynamic-update-slice, f32[1024]{0:T(1024)S(1)} %dynamic-update-slice.1, f32[1024]{0:T(1024)S(1)} %dynamic-update-slice.2), channel_id=2, replica_groups=mesh['ctx'=16,'vocab'=2] {'ctx'}, use_global_device_ids=true, to_apply=%add.1 | all-reduce | flops 3072 | bytes 24576
  202.7 0.7 while.19
  203.4 0.7 multiply_reduce_fusion.3
  204.0 1.1 multiply_convert_fusion
  205.2 5.6 %all_gather.27 = bf16[128,988]{1,0:T(8,128)(2,1)S(1)} all-gather(bf16[64,988]{1,0:T(8,128)(2,1)S(1)} %multiply_convert_fusion), channel_id=1, replica_groups=mesh['ctx'=16,'vocab'=2] {'vocab'}, dimensions={0}, use_global_device_ids=true | all-gather | bytes 379392 | tf_op jit(solution)/shard_map/all_gather | solution.py:101
  210.8 5.9 %fusion.33 = f32[128,4096]{1,0:T(8,128)} fusion(bf16[128,988]{1,0:T(8,128)(2,1)S(1)} %all_gather.27, bf16[988,4096]{1,0:T(8,128)(2,1)} %param.11), kind=kOutput, calls=%fused_computation.119 | convolution fusion | flops 1035993088 | bytes 10443776 | tf_op jit(solution)/shard_map/dot_general | solution.py:106
  216.7 6.8 %convolution_convert_fusion = bf16[988,4096]{1,0:T(8,128)(2,1)} fusion(bf16[128,988]{1,0:T(8,128)(2,1)S(1)} %all_gather.27, bf16[256,4096]{1,0:T(8,128)(2,1)} %copy-done.2, s32[]{:T(128)S(6)} %select_n.206), kind=kOutput, calls=%fused_computation.15 | convolution fusion | flops 1040039936 | bytes 9395204 | tf_op jit(solution)/shard_map/dot_general | solution.py:102
  223.6 51.3 %reduce-scatter.5.cloned.1.call-done = f32[8,4096]{1,0:T(8,128)} async-done(((f32[128,4096]{1,0:T(8,128)}), f32[8,4096]{1,0:T(8,128)}) %reduce-scatter.5.cloned.1.call-update) | async-done | bytes 131088 | tf_op jit(solution)/shard_map/reduce_scatter | solution.py:105
  274.9 1.1 multiply_reduce_fusion
  276.0 5.6 %all-reduce.5 = (f32[]{:T(128)}, f32[8]{0:T(128)S(1)}) all-reduce(f32[]{:T(128)} %get-tuple-element.212, f32[8]{0:T(128)S(1)} %get-tuple-element.188), channel_id=1, replica_groups=mesh['ctx'=16,'vocab'=2] {'vocab'}, use_global_device_ids=true, to_apply=%region_11.12 | all-reduce | flops 9 | bytes 72 | tf_op jit(solution)/shard_map/psum | solution.py:96
  281.6 57.6 %psum.31 = f32[4096]{0:T(1024)} all-reduce(f32[4096]{0:T(1024)S(1)} %get-tuple-element.187), channel_id=1, replica_groups=mesh['ctx'=16,'vocab'=2] {'ctx'}, use_global_device_ids=true, to_apply=%region_17.18 | all-reduce | flops 4096 | bytes 32768 | tf_op jit(solution)/shard_map/psum | solution.py:112
  339.2 2.9 scatter_custom_fusion
  (102 shorter events, 2.4 us)
Async XLA Ops:
  7.2 6.5 %copy-start = (bf16[256,4096]{1,0:T(8,128)(2,1)S(1)}, bf16[256,4096]{1,0:T(8,128)(2,1)}, u32[]{:S(2)}) copy-start(bf16[256,4096]{1,0:T(8,128)(2,1)} %param.9) | copy-start | bytes 6291460
  7.2 110.1 %copy-start.3 = (f32[4096]{0:T(1024)S(1)}, f32[4096]{0:T(1024)}, u32[]{:S(2)}) copy-start(f32[4096]{0:T(1024)} %param.10) | copy-start | bytes 49156
  7.2 131.2 %reduce-scatter.3.cloned.1.call-start = ((), (), s32[]{:S(2)}) async-start(), calls=%async_computation.2 | async-start | bytes 786432 | tf_op jit(solution)/shard_map/reduce_scatter | solution.py:81
  21.2 6.4 %collective-permute-start = (bf16[8,4096]{1,0:T(8,128)(2,1)S(1)}, bf16[8,4096]{1,0:T(8,128)(2,1)S(1)}, u32[]{:S(2)}, u32[]{:S(2)}) collective-permute-start(bf16[8,4096]{1,0:T(8,128)(2,1)S(1)} %multiply_convert_fusion.1), channel_id=1, source_target_pairs={{0,2},{2,4},{4,6},{6,8},{8,10},{10,12},{12,14},{14,16},{16,18},{18... | collective-permute-start | bytes 196616 | tf_op jit(solution)/shard_map/ppermute | solution.py:66
  27.6 6.4 %collective-permute-start.1 = (bf16[8,4096]{1,0:T(8,128)(2,1)S(1)}, bf16[8,4096]{1,0:T(8,128)(2,1)S(1)}, u32[]{:S(2)}, u32[]{:S(2)}) collective-permute-start(bf16[8,4096]{1,0:T(8,128)(2,1)S(1)} %collective-permute-done), channel_id=1, source_target_pairs={{0,2},{2,4},{4,6},{6,8},{8,10},{10,12},{12,14},{14,16},{16,18},{18... | collective-permute-start | bytes 196616 | tf_op jit(solution)/shard_map/ppermute | solution.py:66
  34.0 6.4 %collective-permute-start.2 = (bf16[8,4096]{1,0:T(8,128)(2,1)S(1)}, bf16[8,4096]{1,0:T(8,128)(2,1)S(1)}, u32[]{:S(2)}, u32[]{:S(2)}) collective-permute-start(bf16[8,4096]{1,0:T(8,128)(2,1)S(1)} %collective-permute-done.1), channel_id=1, source_target_pairs={{0,2},{2,4},{4,6},{6,8},{8,10},{10,12},{12,14},{14,16},{16,18},{18... | collective-permute-start | bytes 196616 | tf_op jit(solution)/shard_map/ppermute | solution.py:66
  40.4 6.4 %collective-permute-start.3 = (bf16[8,4096]{1,0:T(8,128)(2,1)S(1)}, bf16[8,4096]{1,0:T(8,128)(2,1)S(1)}, u32[]{:S(2)}, u32[]{:S(2)}) collective-permute-start(bf16[8,4096]{1,0:T(8,128)(2,1)S(1)} %collective-permute-done.2), channel_id=1, source_target_pairs={{0,2},{2,4},{4,6},{6,8},{8,10},{10,12},{12,14},{14,16},{16,18},{18... | collective-permute-start | bytes 196616 | tf_op jit(solution)/shard_map/ppermute | solution.py:66
  46.8 6.4 %collective-permute-start.4 = (bf16[8,4096]{1,0:T(8,128)(2,1)S(1)}, bf16[8,4096]{1,0:T(8,128)(2,1)S(1)}, u32[]{:S(2)}, u32[]{:S(2)}) collective-permute-start(bf16[8,4096]{1,0:T(8,128)(2,1)S(1)} %collective-permute-done.3), channel_id=1, source_target_pairs={{0,2},{2,4},{4,6},{6,8},{8,10},{10,12},{12,14},{14,16},{16,18},{18... | collective-permute-start | bytes 196616 | tf_op jit(solution)/shard_map/ppermute | solution.py:66
  53.2 6.4 %collective-permute-start.5 = (bf16[8,4096]{1,0:T(8,128)(2,1)S(1)}, bf16[8,4096]{1,0:T(8,128)(2,1)S(1)}, u32[]{:S(2)}, u32[]{:S(2)}) collective-permute-start(bf16[8,4096]{1,0:T(8,128)(2,1)S(1)} %collective-permute-done.4), channel_id=1, source_target_pairs={{0,2},{2,4},{4,6},{6,8},{8,10},{10,12},{12,14},{14,16},{16,18},{18... | collective-permute-start | bytes 196616 | tf_op jit(solution)/shard_map/ppermute | solution.py:66
  59.5 6.4 %collective-permute-start.6 = (bf16[8,4096]{1,0:T(8,128)(2,1)S(1)}, bf16[8,4096]{1,0:T(8,128)(2,1)S(1)}, u32[]{:S(2)}, u32[]{:S(2)}) collective-permute-start(bf16[8,4096]{1,0:T(8,128)(2,1)S(1)} %collective-permute-done.5), channel_id=1, source_target_pairs={{0,2},{2,4},{4,6},{6,8},{8,10},{10,12},{12,14},{14,16},{16,18},{18... | collective-permute-start | bytes 196616 | tf_op jit(solution)/shard_map/ppermute | solution.py:66
  65.9 6.4 %collective-permute-start.7 = (bf16[8,4096]{1,0:T(8,128)(2,1)S(1)}, bf16[8,4096]{1,0:T(8,128)(2,1)S(1)}, u32[]{:S(2)}, u32[]{:S(2)}) collective-permute-start(bf16[8,4096]{1,0:T(8,128)(2,1)S(1)} %collective-permute-done.6), channel_id=1, source_target_pairs={{0,2},{2,4},{4,6},{6,8},{8,10},{10,12},{12,14},{14,16},{16,18},{18... | collective-permute-start | bytes 196616 | tf_op jit(solution)/shard_map/ppermute | solution.py:66
  72.3 6.4 %collective-permute-start.8 = (bf16[8,4096]{1,0:T(8,128)(2,1)S(1)}, bf16[8,4096]{1,0:T(8,128)(2,1)S(1)}, u32[]{:S(2)}, u32[]{:S(2)}) collective-permute-start(bf16[8,4096]{1,0:T(8,128)(2,1)S(1)} %collective-permute-done.7), channel_id=1, source_target_pairs={{0,2},{2,4},{4,6},{6,8},{8,10},{10,12},{12,14},{14,16},{16,18},{18... | collective-permute-start | bytes 196616 | tf_op jit(solution)/shard_map/ppermute | solution.py:66
  78.7 6.4 %collective-permute-start.9 = (bf16[8,4096]{1,0:T(8,128)(2,1)S(1)}, bf16[8,4096]{1,0:T(8,128)(2,1)S(1)}, u32[]{:S(2)}, u32[]{:S(2)}) collective-permute-start(bf16[8,4096]{1,0:T(8,128)(2,1)S(1)} %collective-permute-done.8), channel_id=1, source_target_pairs={{0,2},{2,4},{4,6},{6,8},{8,10},{10,12},{12,14},{14,16},{16,18},{18... | collective-permute-start | bytes 196616 | tf_op jit(solution)/shard_map/ppermute | solution.py:66
  85.1 6.4 %collective-permute-start.10 = (bf16[8,4096]{1,0:T(8,128)(2,1)S(1)}, bf16[8,4096]{1,0:T(8,128)(2,1)S(1)}, u32[]{:S(2)}, u32[]{:S(2)}) collective-permute-start(bf16[8,4096]{1,0:T(8,128)(2,1)S(1)} %collective-permute-done.9), channel_id=1, source_target_pairs={{0,2},{2,4},{4,6},{6,8},{8,10},{10,12},{12,14},{14,16},{16,18},{18... | collective-permute-start | bytes 196616 | tf_op jit(solution)/shard_map/ppermute | solution.py:66
  91.5 6.4 %collective-permute-start.11 = (bf16[8,4096]{1,0:T(8,128)(2,1)S(1)}, bf16[8,4096]{1,0:T(8,128)(2,1)S(1)}, u32[]{:S(2)}, u32[]{:S(2)}) collective-permute-start(bf16[8,4096]{1,0:T(8,128)(2,1)S(1)} %collective-permute-done.10), channel_id=1, source_target_pairs={{0,2},{2,4},{4,6},{6,8},{8,10},{10,12},{12,14},{14,16},{16,18},{18... | collective-permute-start | bytes 196616 | tf_op jit(solution)/shard_map/ppermute | solution.py:66
  97.9 6.4 %collective-permute-start.12 = (bf16[8,4096]{1,0:T(8,128)(2,1)S(1)}, bf16[8,4096]{1,0:T(8,128)(2,1)S(1)}, u32[]{:S(2)}, u32[]{:S(2)}) collective-permute-start(bf16[8,4096]{1,0:T(8,128)(2,1)S(1)} %collective-permute-done.11), channel_id=1, source_target_pairs={{0,2},{2,4},{4,6},{6,8},{8,10},{10,12},{12,14},{14,16},{16,18},{18... | collective-permute-start | bytes 196616 | tf_op jit(solution)/shard_map/ppermute | solution.py:66
  104.3 6.4 %collective-permute-start.13 = (bf16[8,4096]{1,0:T(8,128)(2,1)S(1)}, bf16[8,4096]{1,0:T(8,128)(2,1)S(1)}, u32[]{:S(2)}, u32[]{:S(2)}) collective-permute-start(bf16[8,4096]{1,0:T(8,128)(2,1)S(1)} %collective-permute-done.12), channel_id=1, source_target_pairs={{0,2},{2,4},{4,6},{6,8},{8,10},{10,12},{12,14},{14,16},{16,18},{18... | collective-permute-start | bytes 196616 | tf_op jit(solution)/shard_map/ppermute | solution.py:66
  110.6 6.4 %collective-permute-start.14 = (bf16[8,4096]{1,0:T(8,128)(2,1)S(1)}, bf16[8,4096]{1,0:T(8,128)(2,1)S(1)}, u32[]{:S(2)}, u32[]{:S(2)}) collective-permute-start(bf16[8,4096]{1,0:T(8,128)(2,1)S(1)} %collective-permute-done.13), channel_id=1, source_target_pairs={{0,2},{2,4},{4,6},{6,8},{8,10},{10,12},{12,14},{14,16},{16,18},{18... | collective-permute-start | bytes 196616 | tf_op jit(solution)/shard_map/ppermute | solution.py:66
  117.7 1.4 copy-start.2
  119.0 9.9 %copy-start.1 = (s32[2,16]{1,0:T(2,128)S(1)}, s32[2,16]{1,0:T(2,128)}, u32[]{:S(2)}) copy-start(s32[2,16]{1,0:T(2,128)} %param.13) | copy-start | bytes 388
  125.8 4.7 %copy-start.6 = (u32[32]{0:T(128)S(1)}, u32[32]{0:T(128)}, u32[]{:S(2)}) copy-start(u32[32]{0:T(128)} %constant.238) | copy-start | bytes 388
  125.8 6.1 %copy-start.4 = (s32[2]{0:T(128)S(1)}, s32[2]{0:T(128)}, u32[]{:S(2)}) copy-start(s32[2]{0:T(128)} %param.14) | copy-start | bytes 28
  125.8 6.1 %copy-start.5 = (s32[2]{0:T(128)S(1)}, s32[2]{0:T(128)}, u32[]{:S(2)}) copy-start(s32[2]{0:T(128)} %param.15) | copy-start | bytes 28
  125.8 149.1 %reduce-scatter.5.cloned.1.call-start = ((), (), s32[]{:S(2)}) async-start(), calls=%async_computation.3 | async-start | bytes 2228224 | tf_op jit(solution)/shard_map/reduce_scatter | solution.py:105
Sparse Core Ops, SparseCore 0:
  125.9 12.4 reduce-scatter.2
  216.8 58.0 reduce-scatter.4
